TPU v7x, 128 devices: a whole 4x4x4 slice. The times are simulated.
128 devices in a mesh: axial: 4 (over x), azim: 32 (over z, y, core).
Axes of the slice: x: 4, y: 4, z: 4, core: 2. Of those that a mesh axis runs over, the one named last changes fastest.
Arguments:
- density: float32 [64, 256, 512], P(None, 'azim', 'axial'), may hold values from 0.5 to 2
- velocity: float32 [3, 64, 256, 512], P(None, None, 'azim', 'axial'), may hold values from -3 to 3
- pressure: float32 [64, 256, 512], P(None, 'azim', 'axial'), may hold values from 0.4 to 1.5
- axial_metric: float32 [3, 64, 256, 512], P(None, None, 'azim', 'axial'), may hold values from -4 to 4
- azim_metric: float32 [3, 64, 256, 512], P(None, None, 'azim', 'axial'), may hold values from -4 to 4
- volume: float32 [64, 256, 512], P(None, 'azim', 'axial'), may hold values from 0.5 to 2
- radial_term: float32 [5, 64, 256, 512], P(None, None, 'azim', 'axial'), may hold values from -6 to 6
- panel_area: float32 [256, 512], P('azim', 'axial'), may hold values from 0.5 to 2
- observer_ids: int32 [4, 256, 512], P(None, 'azim', 'axial'), may hold values from 0 to 511
- bin_ids: int32 [4, 256, 512], P(None, 'azim', 'axial'), may hold values from 0 to 127
- weight_ids: int32 [4, 256, 512], P(None, 'azim', 'axial'), may hold values from 0 to 255
- bin_weights: float32 [256], replicated, may hold values from 0.2 to 1
Outputs:
- new_state: float32 [5, 64, 256, 512], P(None, None, 'azim', 'axial')
- signals: float32 [512, 128], P(('axial', 'azim'))
All inputs are finite; a program needn't handle non-finite values.
Results may differ from a plain program's by a relative error of at most 0.0003.
Values sent between devices are 32-bit elements; how exact they have to be, the bound alone decides.
A program may use at most 128 MiB of HBM per device.

v0:
```python
import math
import jax
import jax.numpy as jnp
from jax import lax
from jax.sharding import PartitionSpec as P

OBSERVERS = 512
TIME_BINS = 128
GAMMA = 1.4
SECTION = 0.25
DERIV_ALPHA = 1.0 / 3.0
FILTER_ALPHA = 0.499
DERIV_A = 14.0 / 9.0
DERIV_B = 1.0 / 9.0
HIGHEST = lax.Precision.HIGHEST


def padded(cells, sides, width, closed):
    for axis, dim in sides:
        count = lax.axis_size(axis)
        ends = count if closed else count - 1
        head = lax.slice_in_dim(cells, 0, width, axis=dim)
        tail = lax.slice_in_dim(cells, cells.shape[dim] - width, cells.shape[dim], axis=dim)
        cells = jnp.concatenate(
            [
                lax.ppermute(tail, axis, [(i, (i + 1) % count) for i in range(ends)]),
                cells,
                lax.ppermute(head, axis, [((i + 1) % count, i) for i in range(ends)]),
            ],
            axis=dim,
        )
    return cells


def decay_root(alpha):
    return (-1.0 + math.sqrt(1.0 - 4.0 * alpha * alpha)) / (2.0 * alpha)


def signed_power(base, exponent):
    exponent = jnp.asarray(exponent)
    parity = jnp.where(exponent % 2 == 0, 1.0, -1.0)
    return parity * jnp.exp(exponent.astype(jnp.float32) * math.log(-base))


def deriv_side(extended, dim):
    length = extended.shape[dim] - 6

    def cells(offset):
        return lax.slice_in_dim(extended, 3 + offset, 3 + offset + length, axis=dim)

    return 0.5 * DERIV_A * (cells(1) - cells(-1)) + 0.25 * DERIV_B * (cells(2) - cells(-2))


def filter_side(extended, dim):
    length = extended.shape[dim] - 6

    def cells(offset):
        return lax.slice_in_dim(extended, 3 + offset, 3 + offset + length, axis=dim)

    beta = FILTER_ALPHA
    coeffs = [
        (11.0 + 10.0 * beta) / 16.0,
        (15.0 + 34.0 * beta) / 32.0,
        (-3.0 + 6.0 * beta) / 16.0,
        (1.0 - 2.0 * beta) / 32.0,
    ]
    total = coeffs[0] * cells(0)
    for shift in range(1, 4):
        total = total + 0.5 * coeffs[shift] * (cells(shift) + cells(-shift))
    return total


def fluxes(density, velocity, pressure, energy, metric, volume):
    contra = metric[0] * velocity[0] + metric[1] * velocity[1] + metric[2] * velocity[2]
    mass_flow = density * contra
    pieces = [volume * mass_flow]
    for comp in range(3):
        pieces.append(volume * (mass_flow * velocity[comp] + metric[comp] * pressure))
    pieces.append(volume * (energy + pressure) * contra)
    return jnp.stack(pieces)


def pad_axial(field):
    return padded(field, (("axial", 3),), 3, False)


def pad_azimuth(field):
    return padded(field, (("azim", 2),), 3, True)


def open_line(rhs, alpha):
    base = decay_root(alpha)
    factor_g = -alpha / base
    scale = 1.0 / (factor_g * (1.0 - base * base))
    width_here = rhs.shape[3]
    group_size = lax.axis_size("axial")
    device_pos = lax.axis_index("axial")
    total_len = width_here * group_size
    offsets = jnp.arange(width_here, dtype=jnp.int32)
    local_matrix = signed_power(base, jnp.abs(offsets[:, None] - offsets[None, :]))
    local_part = jnp.einsum("vraj,ij->vrai", rhs, local_matrix, precision=HIGHEST)
    first_moment = jnp.einsum(
        "vraj,j->vra", rhs, signed_power(base, width_here - 1 - offsets), precision=HIGHEST
    )
    last_moment = jnp.einsum("vraj,j->vra", rhs, signed_power(base, offsets), precision=HIGHEST)
    moments = jnp.stack([first_moment, last_moment])[None]
    piece = lax.all_gather(moments, "axial", axis=0, tiled=True)
    others = jnp.arange(piece.shape[0], dtype=jnp.int32)
    gap_up = device_pos - others
    w_left = jnp.where(
        gap_up > 0, signed_power(base, width_here * jnp.maximum(gap_up - 1, 0) + 1), 0.0
    )
    w_right = jnp.where(
        gap_up < 0, signed_power(base, width_here * jnp.maximum(-gap_up - 1, 0) + 1), 0.0
    )
    w_end = signed_power(base, width_here * (group_size - 1 - others))
    left_sum = jnp.einsum("k,kvra->vra", w_left, piece[:, 0], precision=HIGHEST)
    right_sum = jnp.einsum("k,kvra->vra", w_right, piece[:, 1], precision=HIGHEST)
    end_sum = jnp.einsum("k,kvra->vra", w_end, piece[:, 0], precision=HIGHEST)
    left_sum, right_sum, end_sum = (left_sum, right_sum, end_sum)
    position = device_pos * width_here + offsets
    result = local_part + signed_power(base, offsets) * left_sum[..., None]
    result = result + signed_power(base, width_here - 1 - offsets) * right_sum[..., None]
    result = result - signed_power(base, total_len + 1 - position) * end_sum[..., None]
    return scale * result


def cycle_line(rhs, alpha):
    base = decay_root(alpha)
    factor_g = -alpha / base
    width_here = rhs.shape[2]
    group_size = lax.axis_size("azim")
    device_pos = lax.axis_index("azim")
    total_len = width_here * group_size
    scale = 1.0 / (factor_g * (1.0 - base * base) * (1.0 - base**total_len))
    offsets = jnp.arange(width_here, dtype=jnp.int32)
    gap = jnp.abs(offsets[:, None] - offsets[None, :])
    local_matrix = scale * (signed_power(base, gap) + signed_power(base, total_len - gap))
    local_part = jnp.einsum("vrjx,ij->vrix", rhs, local_matrix, precision=HIGHEST)
    first_moment = jnp.einsum(
        "vrjx,j->vrx", rhs, signed_power(base, width_here - 1 - offsets), precision=HIGHEST
    )
    last_moment = jnp.einsum("vrjx,j->vrx", rhs, signed_power(base, offsets), precision=HIGHEST)
    moments = jnp.stack([first_moment, last_moment])[None]
    piece = lax.all_gather(moments, "azim", axis=0, tiled=True)
    others = jnp.arange(piece.shape[0], dtype=jnp.int32)
    shift = (device_pos - others) % group_size
    w_first = jnp.where(
        shift > 0, signed_power(base, width_here * jnp.maximum(shift - 1, 0) + 1), 0.0
    )
    w_last = jnp.where(
        shift > 0, signed_power(base, width_here * jnp.maximum(group_size - shift - 1, 0) + 1), 0.0
    )
    first_sum = jnp.einsum("k,kvrx->vrx", w_first, piece[:, 0], precision=HIGHEST)
    last_sum = jnp.einsum("k,kvrx->vrx", w_last, piece[:, 1], precision=HIGHEST)
    outer = signed_power(base, offsets)[:, None] * first_sum[:, :, None, :]
    outer = outer + signed_power(base, width_here - 1 - offsets)[:, None] * last_sum[:, :, None, :]
    return local_part + scale * outer


def per_device(
    density,
    velocity,
    pressure,
    axial_metric,
    azim_metric,
    volume,
    radial_term,
    panel_area,
    observer_ids,
    bin_ids,
    weight_ids,
    bin_weights,
):
    energy = pressure / (GAMMA - 1.0) + 0.5 * density * (
        velocity[0] ** 2 + velocity[1] ** 2 + velocity[2] ** 2
    )
    state = jnp.concatenate([density[None], density[None] * velocity, energy[None]], axis=0)
    axial_flux = fluxes(density, velocity, pressure, energy, axial_metric, volume)
    azim_flux = fluxes(density, velocity, pressure, energy, azim_metric, volume)
    axial_deriv = open_line(deriv_side(pad_axial(axial_flux), 3), DERIV_ALPHA)
    azim_deriv = cycle_line(deriv_side(pad_azimuth(azim_flux), 2), DERIV_ALPHA)
    sectioned = state + SECTION * (radial_term - (axial_deriv + azim_deriv) / volume)
    smoothed = open_line(filter_side(pad_axial(sectioned), 3), FILTER_ALPHA)
    new_state = cycle_line(filter_side(pad_azimuth(smoothed), 2), FILTER_ALPHA)
    surface = new_state[:, 0]
    source = panel_area * (surface[2] + surface[0] - 1.0)
    table_size = bin_weights.shape[0]
    one_hot = (
        weight_ids.reshape(-1)[:, None] == jnp.arange(table_size, dtype=jnp.int32)[None, :]
    ).astype(jnp.float32)
    entry_weight = jnp.dot(one_hot, bin_weights, precision=HIGHEST)
    values = entry_weight * jnp.broadcast_to(source[None], weight_ids.shape).reshape(-1)
    bucket = (observer_ids * TIME_BINS + bin_ids).reshape(-1)
    partial_signals = jax.ops.segment_sum(
        values, bucket, num_segments=OBSERVERS * TIME_BINS
    ).reshape(OBSERVERS, TIME_BINS)
    signals = lax.psum_scatter(partial_signals, ("axial", "azim"), scatter_dimension=0, tiled=True)
    return (new_state, signals)


def solution(mesh):
    placed = (
        P(None, "azim", "axial"),
        P(None, None, "azim", "axial"),
        P(None, "azim", "axial"),
        P(None, None, "azim", "axial"),
        P(None, None, "azim", "axial"),
        P(None, "azim", "axial"),
        P(None, None, "azim", "axial"),
        P("azim", "axial"),
        P(None, "azim", "axial"),
        P(None, "azim", "axial"),
        P(None, "azim", "axial"),
        P(),
    )
    return jax.shard_map(
        per_device,
        mesh=mesh,
        in_specs=placed,
        out_specs=(P(None, None, "azim", "axial"), P(("axial", "azim"), None)),
        check_vma=False,
    )
```

profile of v0, /device:TPU:1, one launch (start us, length us, event | category | flops | bytes accessed | tf_op | source)
XLA Modules:
  0.0 457.5 jit_solution(16983114548345051890)
XLA Ops:
  7.3 2.7 bitcast_dynamic-update-slice_fusion.4
  15.6 6.4 %collective-permute-done.2 = f32[5,64,3,128]{3,1,2,0:T(8,128)S(1)} collective-permute-done((f32[5,64,3,128]{3,1,2,0:T(8,128)S(1)}, f32[5,64,3,128]{3,1,2,0:T(8,128)S(1)}, u32[]{:S(2)}, u32[]{:S(2)}) %collective-permute-start.2) | collective-permute-done | bytes 491552 | tf_op jit(solution)/shard_map/ppermute | solution.py:28
  32.8 4.2 collective-permute-start.1
  42.7 5.7 %fusion.30 = f32[5,64,8,128]{3,2,1,0:T(8,128)S(1)} fusion(f32[5,64,8,3]{3,2,1,0:T(8,128)} %copy.17, f32[5,64,8,128]{3,2,1,0:T(8,128)S(1)} %bitcast_dynamic-update-slice_fusion.5, f32[5,64,8,3]{3,2,1,0:T(8,128)} %copy.15), kind=kLoop, calls=%fused_computation.64 | loop fusion | flops 2949120 | bytes 2682880 | tf_op jit(solution)/shard_map/add | solution.py:51
  48.3 17.3 %fusion.215 = f32[1,5,64,8]{3,0,2,1:T(1,128)S(1)} fusion(f32[5,64,8,128]{3,2,1,0:T(8,128)S(1)} %fusion.30), kind=kOutput, calls=%fused_computation.350 | convolution fusion | flops 3934336 | bytes 1320960 | tf_op jit(solution)/shard_map/vraj,j->vra/dot_general | solution.py:102
  65.7 17.7 %fusion.213 = f32[1,5,64,8]{3,0,2,1:T(1,128)S(1)} fusion(f32[5,64,8,128]{3,2,1,0:T(8,128)S(1)} %fusion.30), kind=kOutput, calls=%fused_computation.348 | convolution fusion | flops 3933568 | bytes 1320960 | tf_op jit(solution)/shard_map/vraj,j->vra/dot_general | solution.py:105
  83.5 9.9 %all-gather = f32[8,5,64,8]{2,3,1,0:T(8,128)S(1)} all-gather(f32[2,5,64,8]{2,3,1,0:T(8,128)S(1)} %pad_maximum_fusion.10), channel_id=2, replica_groups=mesh['axial'=4,'azim'=32] {'axial'}, dimensions={0}, use_global_device_ids=true | all-gather | bytes 102400 | tf_op jit(solution)/shard_map/all_gather | solution.py:107
  94.7 2.5 fusion.19
  97.3 5.2 %slice_bitcast_fusion.3 = (f32[32,5,64,128]{3,2,1,0:T(8,128)S(1)}, f32[32,5,64,128]{3,2,1,0:T(8,128)S(1)}) fusion(f32[32,2,5,64,128]{4,3,2,1,0:T(8,128)} %bitcast.355), kind=kLoop, calls=%fused_computation.4 | loop fusion | bytes 20971520 | tf_op jit(solution)/shard_map/squeeze | solution.py:154
  102.5 5.4 %fusion.6 = f32[1,5,64,128]{3,0,2,1:T(1,128)S(1)} fusion(f32[32,5,64,128]{3,2,1,0:T(8,128)S(1)} %get-tuple-element.12, s32[]{:T(128)S(6)} %axis_index.33), kind=kOutput, calls=%fused_computation.11 | convolution fusion | flops 15729728 | bytes 5406724 | tf_op jit(solution)/shard_map/k,kvrx->vrx/dot_general | solution.py:154
  108.0 5.6 %fusion.4 = f32[1,5,64,128]{3,0,2,1:T(1,128)S(1)} fusion(f32[32,5,64,128]{3,2,1,0:T(8,128)S(1)} %get-tuple-element.13, s32[]{:T(128)S(6)} %axis_index.33), kind=kOutput, calls=%fused_computation.9 | convolution fusion | flops 15729728 | bytes 5406724 | tf_op jit(solution)/shard_map/k,kvrx->vrx/dot_general | solution.py:155
  120.5 4.0 collective-permute-start.5
  127.7 6.2 %fusion.47 = f32[5,64,8,128]{3,2,1,0:T(8,128)S(1)} fusion(f32[5,64,8,3]{3,2,1,0:T(8,128)} %copy.25, f32[5,64,8,128]{3,2,1,0:T(8,128)S(1)} %fusion.21, f32[5,64,8,3]{3,2,1,0:T(8,128)} %copy.23), kind=kLoop, calls=%fused_computation.81 | loop fusion | flops 5242880 | bytes 2682880 | tf_op jit(solution)/shard_map/add | solution.py:69
  133.8 17.3 %fusion.204 = f32[1,5,64,8]{3,0,2,1:T(1,128)S(1)} fusion(f32[5,64,8,128]{3,2,1,0:T(8,128)S(1)} %fusion.47), kind=kOutput, calls=%fused_computation.339 | convolution fusion | flops 3934336 | bytes 1320960 | tf_op jit(solution)/shard_map/vraj,j->vra/dot_general | solution.py:102
  151.1 17.7 %fusion.202 = f32[1,5,64,8]{3,0,2,1:T(1,128)S(1)} fusion(f32[5,64,8,128]{3,2,1,0:T(8,128)S(1)} %fusion.47), kind=kOutput, calls=%fused_computation.337 | convolution fusion | flops 3933568 | bytes 1320960 | tf_op jit(solution)/shard_map/vraj,j->vra/dot_general | solution.py:105
  169.0 9.2 %all-gather.2 = f32[8,5,64,8]{2,3,1,0:T(8,128)S(1)} all-gather(f32[2,5,64,8]{2,3,1,0:T(8,128)S(1)} %pad_maximum_fusion.11), channel_id=4, replica_groups=mesh['axial'=4,'azim'=32] {'axial'}, dimensions={0}, use_global_device_ids=true | all-gather | bytes 102400 | tf_op jit(solution)/shard_map/all_gather | solution.py:107
  181.4 16.4 %collective-permute-start.6 = (f32[5,64,3,128]{3,1,2,0:T(8,128)S(1)}, f32[5,64,3,128]{3,1,2,0:T(8,128)S(1)}, u32[]{:S(2)}, u32[]{:S(2)}) collective-permute-start(f32[5,64,3,128]{3,1,2,0:T(8,128)S(1)} %copy.26), channel_id=1, source_target_pairs={{1,0},{2,1},{3,2},{4,3},{5,4},{6,5},{7,6},{8,7},{9,8},{10,9},{11,1... | collective-permute-start | bytes 1474568 | tf_op jit(solution)/shard_map/ppermute | solution.py:28
  199.6 4.1 collective-permute-done.7
  211.5 56.8 %all-gather.9.cloned.1.call-done = f32[64,5,64,128]{3,2,1,0:T(8,128)} async-done(((f32[2,5,64,128]{3,2,1,0:T(8,128)}), f32[64,5,64,128]{3,2,1,0:T(8,128)}) %all-gather.9.cloned.1.call-update) | async-done | bytes 10485776 | tf_op jit(solution)/shard_map/all_gather | solution.py:145
  268.3 5.2 %slice_bitcast_fusion.1 = (f32[32,5,64,128]{3,2,1,0:T(8,128)S(1)}, f32[32,5,64,128]{3,2,1,0:T(8,128)S(1)}) fusion(f32[32,2,5,64,128]{4,3,2,1,0:T(8,128)} %bitcast.356), kind=kLoop, calls=%fused_computation.2 | loop fusion | bytes 20971520 | tf_op jit(solution)/shard_map/squeeze | solution.py:154
  273.5 5.4 %fusion.2 = f32[1,5,64,128]{3,0,2,1:T(1,128)S(1)} fusion(f32[32,5,64,128]{3,2,1,0:T(8,128)S(1)} %get-tuple-element.10, s32[]{:T(128)S(6)} %axis_index.33), kind=kOutput, calls=%fused_computation.7 | convolution fusion | flops 15729728 | bytes 5406724 | tf_op jit(solution)/shard_map/k,kvrx->vrx/dot_general | solution.py:154
  278.9 5.6 %fusion = f32[1,5,64,128]{3,0,2,1:T(1,128)S(1)} fusion(f32[32,5,64,128]{3,2,1,0:T(8,128)S(1)} %get-tuple-element.11, s32[]{:T(128)S(6)} %axis_index.33), kind=kOutput, calls=%fused_computation.5 | convolution fusion | flops 15729728 | bytes 5406724 | tf_op jit(solution)/shard_map/k,kvrx->vrx/dot_general | solution.py:155
  286.0 22.6 %scatter_custom_fusion = f32[65536]{0:T(1024)} fusion(s32[4096]{0:T(1024)S(1)} %add_bitcast_fusion, f32[4096]{0:T(1024)S(1)} %bitcast_multiply_fusion.21, f32[]{:T(128)} %constant.254.clone.1), kind=kCustom, calls=%fused_computation.160 | custom fusion | flops 4096 | bytes 262148 | tf_op jit(solution)/shard_map/scatter-add | solution.py:195
  308.6 140.8 %all-reduce.3.cloned.1.call-done = f32[512,128]{1,0:T(8,128)} async-done(((f32[512,128]{1,0:T(8,128)}), f32[512,128]{1,0:T(8,128)}) %all-reduce.3.cloned.1.call-update) | async-done | bytes 262160
  (132 shorter events, 49.0 us)
Async XLA Ops:
  7.2 201.9 %copy-start = (f32[256]{0:T(256)S(1)}, f32[256]{0:T(256)}, u32[]{:S(2)}) copy-start(f32[256]{0:T(256)} %param.23) | copy-start | bytes 3076
  7.2 90.1 %all-gather.7.cloned.1.call-start = ((), (), s32[]{:S(2)}) async-start(), calls=%async_computation | async-start | bytes 10813440 | tf_op jit(solution)/shard_map/all_gather | solution.py:145
  12.4 14.7 %copy-start.12 = (f32[64,8,128]{2,1,0:T(8,128)}, f32[64,8,128]{2,1,0:T(8,128)S(1)}, u32[]{:S(2)}) copy-start(f32[64,8,128]{2,1,0:T(8,128)S(1)} %get-tuple-element.3) | copy-start | bytes 786436
  12.7 9.3 %collective-permute-start.2 = (f32[5,64,3,128]{3,1,2,0:T(8,128)S(1)}, f32[5,64,3,128]{3,1,2,0:T(8,128)S(1)}, u32[]{:S(2)}, u32[]{:S(2)}) collective-permute-start(f32[5,64,3,128]{3,1,2,0:T(8,128)S(1)} %copy.18), channel_id=1, source_target_pairs={{1,0},{2,1},{3,2},{4,3},{5,4},{6,5},{7,6},{8,7},{9,8},{10,9},{11,1... | collective-permute-start | bytes 1474568 | tf_op jit(solution)/shard_map/ppermute | solution.py:28
  14.2 8.1 %collective-permute-start.3 = (f32[5,64,3,128]{3,1,2,0:T(8,128)S(1)}, f32[5,64,3,128]{3,1,2,0:T(8,128)S(1)}, u32[]{:S(2)}, u32[]{:S(2)}) collective-permute-start(f32[5,64,3,128]{3,1,2,0:T(8,128)S(1)} %copy.20), channel_id=1, source_target_pairs={{0,1},{1,2},{2,3},{3,4},{4,5},{5,6},{6,7},{7,8},{8,9},{9,10},{10,1... | collective-permute-start | bytes 1474568 | tf_op jit(solution)/shard_map/ppermute | solution.py:26
  27.1 241.2 %all-gather.9.cloned.1.call-start = ((), (), s32[]{:S(2)}) async-start(), calls=%async_computation.1 | async-start | bytes 10813440 | tf_op jit(solution)/shard_map/all_gather | solution.py:145
  30.4 9.1 %collective-permute-start = (f32[5,64,8,3]{1,2,3,0:T(8,128)S(1)}, f32[5,64,8,3]{1,2,3,0:T(8,128)S(1)}, u32[]{:S(2)}, u32[]{:S(2)}) collective-permute-start(f32[5,64,8,3]{1,2,3,0:T(8,128)S(1)} %copy.14), channel_id=1, source_target_pairs={{32,0},{64,32},{96,64},{33,1},{65,33},{97,65},{34,2},{66,34},{98,6... | collective-permute-start | bytes 92168 | tf_op jit(solution)/shard_map/ppermute | solution.py:28
  32.8 8.3 %collective-permute-start.1 = (f32[5,64,8,3]{1,2,3,0:T(8,128)}, f32[5,64,8,3]{1,2,3,0:T(8,128)S(1)}, u32[]{:S(2)}, u32[]{:S(2)}) collective-permute-start(f32[5,64,8,3]{1,2,3,0:T(8,128)} %copy.16), channel_id=1, source_target_pairs={{0,32},{32,64},{64,96},{1,33},{33,65},{65,97},{2,34},{34,66},{66,9... | collective-permute-start | bytes 92168 | tf_op jit(solution)/shard_map/ppermute | solution.py:26
  102.5 11.1 %copy-start.22 = (f32[5,64,8,128]{3,2,1,0:T(8,128)S(1)}, f32[5,64,8,128]{3,2,1,0:T(8,128)}, u32[]{:S(2)}) copy-start(f32[5,64,8,128]{3,2,1,0:T(8,128)} %fusion.19) | copy-start | bytes 3932164
  107.9 5.7 %copy-start.3 = (f32[5,64,8,128]{3,2,1,0:T(8,128)S(1)}, f32[5,64,8,128]{3,2,1,0:T(8,128)}, u32[]{:S(2)}) copy-start(f32[5,64,8,128]{3,2,1,0:T(8,128)} %copy-done.2) | copy-start | bytes 3932164
  107.9 5.7 %copy-start.5 = (f32[64,8,128]{2,1,0:T(8,128)S(1)}, f32[64,8,128]{2,1,0:T(8,128)}, u32[]{:S(2)}) copy-start(f32[64,8,128]{2,1,0:T(8,128)} %param.17) | copy-start | bytes 786436
  107.9 5.7 %copy-start.10 = (f32[64,8,128]{2,1,0:T(8,128)S(1)}, f32[64,8,128]{2,1,0:T(8,128)}, u32[]{:S(2)}) copy-start(f32[64,8,128]{2,1,0:T(8,128)} %param.12) | copy-start | bytes 786436
  107.9 5.7 %copy-start.13 = (f32[64,8,128]{2,1,0:T(8,128)S(1)}, f32[64,8,128]{2,1,0:T(8,128)}, u32[]{:S(2)}) copy-start(f32[64,8,128]{2,1,0:T(8,128)} %copy-done.12) | copy-start | bytes 786436
  107.9 5.7 %copy-start.15 = (f32[3,64,8,128]{3,2,1,0:T(8,128)S(1)}, f32[3,64,8,128]{3,2,1,0:T(8,128)}, u32[]{:S(2)}) copy-start(f32[3,64,8,128]{3,2,1,0:T(8,128)} %broadcast_multiply_fusion.1) | copy-start | bytes 2359300
  108.0 5.7 %copy-start.19 = (f32[5,64,8,128]{3,2,1,0:T(8,128)S(1)}, f32[5,64,8,128]{3,2,1,0:T(8,128)}, u32[]{:S(2)}) copy-start(f32[5,64,8,128]{3,2,1,0:T(8,128)} %param.18) | copy-start | bytes 3932164
  108.0 5.7 %copy-start.21 = (f32[8]{0:T(128)S(1)}, f32[8]{0:T(128)}, u32[]{:S(2)}) copy-start(f32[8]{0:T(128)} %get-tuple-element.39) | copy-start | bytes 100
  118.7 5.8 %collective-permute-start.4 = (f32[5,64,8,3]{1,2,3,0:T(8,128)S(1)}, f32[5,64,8,3]{1,2,3,0:T(8,128)S(1)}, u32[]{:S(2)}, u32[]{:S(2)}) collective-permute-start(f32[5,64,8,3]{1,2,3,0:T(8,128)S(1)} %copy.22), channel_id=1, source_target_pairs={{32,0},{64,32},{96,64},{33,1},{65,33},{97,65},{34,2},{66,34},{98,6... | collective-permute-start | bytes 92168 | tf_op jit(solution)/shard_map/ppermute | solution.py:28
  120.5 5.6 %collective-permute-start.5 = (f32[5,64,8,3]{1,2,3,0:T(8,128)S(1)}, f32[5,64,8,3]{1,2,3,0:T(8,128)S(1)}, u32[]{:S(2)}, u32[]{:S(2)}) collective-permute-start(f32[5,64,8,3]{1,2,3,0:T(8,128)S(1)} %copy.24), channel_id=1, source_target_pairs={{0,32},{32,64},{64,96},{1,33},{33,65},{65,97},{2,34},{34,66},{66,9... | collective-permute-start | bytes 92168 | tf_op jit(solution)/shard_map/ppermute | solution.py:26
  181.4 17.9 %collective-permute-start.6 = (f32[5,64,3,128]{3,1,2,0:T(8,128)S(1)}, f32[5,64,3,128]{3,1,2,0:T(8,128)S(1)}, u32[]{:S(2)}, u32[]{:S(2)}) collective-permute-start(f32[5,64,3,128]{3,1,2,0:T(8,128)S(1)} %copy.26), channel_id=1, source_target_pairs={{1,0},{2,1},{3,2},{4,3},{5,4},{6,5},{7,6},{8,7},{9,8},{10,9},{11,1... | collective-permute-start | bytes 1474568 | tf_op jit(solution)/shard_map/ppermute | solution.py:28
  197.8 5.8 %collective-permute-start.7 = (f32[5,64,3,128]{3,1,2,0:T(8,128)S(1)}, f32[5,64,3,128]{3,1,2,0:T(8,128)S(1)}, u32[]{:S(2)}, u32[]{:S(2)}) collective-permute-start(f32[5,64,3,128]{3,1,2,0:T(8,128)S(1)} %copy.28), channel_id=1, source_target_pairs={{0,1},{1,2},{2,3},{3,4},{4,5},{5,6},{6,7},{7,8},{8,9},{9,10},{10,1... | collective-permute-start | bytes 1474568 | tf_op jit(solution)/shard_map/ppermute | solution.py:26
  208.2 3.2 copy-start.16
  208.2 3.2 copy-start.17
  209.0 240.4 %all-reduce.3.cloned.1.call-start = ((), (), s32[]{:S(2)}) async-start(), calls=%async_computation.2 | async-start | bytes 524288
  286.0 164.7 %copy-start.11 = (f32[5,64,8,128]{3,2,1,0:T(8,128)}, f32[5,64,8,128]{3,2,1,0:T(8,128)S(1)}, u32[]{:S(2)}) copy-start(f32[5,64,8,128]{3,2,1,0:T(8,128)S(1)} %fusion.17) | copy-start | bytes 3932164
  (10 other events, 21.5 us)
Sparse Core Ops, SparseCore 0:
  27.2 63.5 all-gather.6
  209.2 59.0 all-gather.8
  308.8 140.6 all-reduce.2
where the time goes:
time: 464 us; the launch traced here: 457 us
  waiting for transfers between devices  209 us (45%)
  matrix products  108 us (23%)
  other arithmetic  44.7 us (10%)
  local copies, waits for them, and re-layouts  30.9 us (7%)
  starting transfers between devices  30.1 us (6%)
  blocking collectives  19.1 us (4%)
  between operations  14.7 us (3%)
    unnamed x4, waiting for transfers between devices  141 us
    all_gather x2, waiting for transfers between devices, cycle_line(): piece = lax.all_gather(moments, 'azim', axis=0, tiled=True)  56.8 us
    dot_general x2, matrix products, open_line(): jnp.einsum('vraj,j->vra', rhs, signed_power(base, offsets), precision=HIG...  35.4 us
    dot_general x2, matrix products, open_line(): jnp.einsum('vraj,j->vra', rhs, signed_power(base, width_here - 1 - offset...  34.6 us
    scatter-add x1, other arithmetic, per_device(): jax.ops.segment_sum(values, bucket, num_segments=OBSERVERS * TIME_BINS)  22.6 us
    ppermute x4, starting transfers between devices, padded(): lax.ppermute(head, axis, [((i + 1) % count, i) for i in range(ends)])  20.4 us
    all_gather x2, blocking collectives, open_line(): piece = lax.all_gather(moments, 'axial', axis=0, tiled=True)  19.1 us
    dot_general x2, matrix products, cycle_line(): last_sum = jnp.einsum('k,kvrx->vrx', w_last, piece[:, 1], precision=HIGHEST)  11.2 us
  transfers between devices with their start and end apart: 11, of which 5 were waited for; matrix products, arithmetic and copies ran while one was open for 13% of the time, Pallas kernels for 0%

commit v1 on v0

--- a/solution.py
+++ b/solution.py
@@ -142,7 +142,9 @@
     )
     last_moment = jnp.einsum("vrjx,j->vrx", rhs, signed_power(base, offsets), precision=HIGHEST)
     moments = jnp.stack([first_moment, last_moment])[None]
-    piece = lax.all_gather(moments, "azim", axis=0, tiled=True)
+    piece = jnp.concatenate(
+        lax.all_to_all(jnp.stack([moments] * lax.axis_size("azim")), "azim", 0, 0), axis=0
+    )
     others = jnp.arange(piece.shape[0], dtype=jnp.int32)
     shift = (device_pos - others) % group_size
     w_first = jnp.where(

time: 464 us -> 620 us (1.34)
  waiting for transfers between devices: 209 us -> 334 us
  starting transfers between devices: 30.1 us -> 50.7 us
  local copies, waits for them, and re-layouts: 30.9 us -> 41.3 us
    all_to_all x0 -> x2, waiting for transfers between devices: none -> 177 us  [cycle_line(): lax.all_to_all(jnp.stack([moments] * lax.axis_size('azim')), 'azim', 0, 0)]
    all_gather x2 -> x0, waiting for transfers between devices: 56.8 us -> none  [cycle_line(): piece = lax.all_gather(moments, 'azim', axis=0, tiled=True)]
    all_to_all x0 -> x2, starting transfers between devices: none -> 24.7 us  [cycle_line(): lax.all_to_all(jnp.stack([moments] * lax.axis_size('azim')), 'azim', 0, 0)]
    another operation x0 -> x2, local copies, waits for them, and re-layouts: none -> 10.4 us  [cycle_line(): jnp.stack([moments] * lax.axis_size('azim'))]
    unnamed x4 -> x2, waiting for transfers between devices: 141 us -> 145 us
  transfers between devices with their start and end apart: 11 -> 11, of which waited for: 5 -> 6; matrix products, arithmetic and copies ran while one was open for 13% -> 10% of each run, Pallas kernels for 0% -> 0%
where the time goes in v1:
time: 620 us; the launch traced here: 613 us
  waiting for transfers between devices  334 us (54%)
  matrix products  108 us (17%)
  starting transfers between devices  50.7 us (8%)
  other arithmetic  42.6 us (7%)
  local copies, waits for them, and re-layouts  41.3 us (7%)
  blocking collectives  20.5 us (3%)
  between operations  15 us (2%)
    all_to_all x2, waiting for transfers between devices, cycle_line(): lax.all_to_all(jnp.stack([moments] * lax.axis_size('azim')), 'azim', 0, 0)  177 us
    unnamed x2, waiting for transfers between devices  145 us
    dot_general x2, matrix products, open_line(): jnp.einsum('vraj,j->vra', rhs, signed_power(base, offsets), precision=HIG...  35.4 us
    dot_general x2, matrix products, open_line(): jnp.einsum('vraj,j->vra', rhs, signed_power(base, width_here - 1 - offset...  34.6 us
    all_to_all x2, starting transfers between devices, cycle_line(): lax.all_to_all(jnp.stack([moments] * lax.axis_size('azim')), 'azim', 0, 0)  24.7 us
    scatter-add x1, other arithmetic, per_device(): jax.ops.segment_sum(values, bucket, num_segments=OBSERVERS * TIME_BINS)  22.6 us
    all_gather x2, blocking collectives, open_line(): piece = lax.all_gather(moments, 'axial', axis=0, tiled=True)  20.5 us
    ppermute x4, starting transfers between devices, padded(): lax.ppermute(head, axis, [((i + 1) % count, i) for i in range(ends)])  16.4 us
  transfers between devices with their start and end apart: 11, of which 6 were waited for; matrix products, arithmetic and copies ran while one was open for 10% of the time, Pallas kernels for 0%

profile of v1, /device:TPU:1, one launch (start us, length us, event | category | flops | bytes accessed | tf_op | source)
XLA Modules:
  0.0 612.8 jit_solution(5007748619897243049)
XLA Ops:
  14.9 6.4 %collective-permute-done.2 = f32[5,64,3,128]{3,1,2,0:T(8,128)S(1)} collective-permute-done((f32[5,64,3,128]{3,1,2,0:T(8,128)S(1)}, f32[5,64,3,128]{3,1,2,0:T(8,128)S(1)}, u32[]{:S(2)}, u32[]{:S(2)}) %collective-permute-start.2) | collective-permute-done | bytes 491552 | tf_op jit(solution)/shard_map/ppermute | solution.py:28
  25.6 5.2 stack.96
  30.8 14.2 %all-to-all-start = ((f32[32,1,2,5,64,128]{5,4,3,2,1,0:T(8,128)}), f32[32,1,2,5,64,128]{5,4,3,2,1,0:T(8,128)}, u32[]{:S(2)}, u32[]{:S(2)}) async-start(f32[32,1,2,5,64,128]{5,4,3,2,1,0:T(8,128)} %stack.96), calls=%async_computation | async-start | bytes 20971520 | tf_op jit(solution)/shard_map/all_to_all | solution.py:146
  60.5 5.6 fusion.30
  66.1 17.3 %fusion.215 = f32[1,5,64,8]{3,0,2,1:T(1,128)S(1)} fusion(f32[5,64,8,128]{3,2,1,0:T(8,128)S(1)} %fusion.30), kind=kOutput, calls=%fused_computation.350 | convolution fusion | flops 3934336 | bytes 1320960 | tf_op jit(solution)/shard_map/vraj,j->vra/dot_general | solution.py:102
  83.6 17.7 %fusion.213 = f32[1,5,64,8]{3,0,2,1:T(1,128)S(1)} fusion(f32[5,64,8,128]{3,2,1,0:T(8,128)S(1)} %fusion.30), kind=kOutput, calls=%fused_computation.348 | convolution fusion | flops 3933568 | bytes 1320960 | tf_op jit(solution)/shard_map/vraj,j->vra/dot_general | solution.py:105
  101.4 10.7 %all-gather = f32[8,5,64,8]{2,3,1,0:T(8,128)S(1)} all-gather(f32[2,5,64,8]{2,3,1,0:T(8,128)S(1)} %pad_maximum_fusion.10), channel_id=2, replica_groups=mesh['axial'=4,'azim'=32] {'axial'}, dimensions={0}, use_global_device_ids=true | all-gather | bytes 102400 | tf_op jit(solution)/shard_map/all_gather | solution.py:107
  115.9 54.4 %all-to-all-done = f32[32,1,2,5,64,128]{5,4,3,2,1,0:T(8,128)} async-done(((f32[32,1,2,5,64,128]{5,4,3,2,1,0:T(8,128)}), f32[32,1,2,5,64,128]{5,4,3,2,1,0:T(8,128)}, u32[]{:S(2)}, u32[]{:S(2)}) %all-to-all-start) | async-done | bytes 10485792 | tf_op jit(solution)/shard_map/all_to_all | solution.py:146
  170.3 5.2 slice_bitcast_fusion.3
  175.5 5.4 fusion.6
  181.0 5.6 fusion.4
  200.6 6.2 %fusion.47 = f32[5,64,8,128]{3,2,1,0:T(8,128)S(1)} fusion(f32[5,64,8,3]{3,2,1,0:T(8,128)} %copy.25, f32[5,64,8,128]{3,2,1,0:T(8,128)S(1)} %fusion.21, f32[5,64,8,3]{3,2,1,0:T(8,128)} %copy.23), kind=kLoop, calls=%fused_computation.81 | loop fusion | flops 5242880 | bytes 2682880 | tf_op jit(solution)/shard_map/add | solution.py:69
  206.9 17.3 %fusion.204 = f32[1,5,64,8]{3,0,2,1:T(1,128)S(1)} fusion(f32[5,64,8,128]{3,2,1,0:T(8,128)S(1)} %fusion.47), kind=kOutput, calls=%fused_computation.339 | convolution fusion | flops 3934336 | bytes 1320960 | tf_op jit(solution)/shard_map/vraj,j->vra/dot_general | solution.py:102
  224.1 17.7 %fusion.202 = f32[1,5,64,8]{3,0,2,1:T(1,128)S(1)} fusion(f32[5,64,8,128]{3,2,1,0:T(8,128)S(1)} %fusion.47), kind=kOutput, calls=%fused_computation.337 | convolution fusion | flops 3933568 | bytes 1320960 | tf_op jit(solution)/shard_map/vraj,j->vra/dot_general | solution.py:105
  242.1 9.7 %all-gather.1 = f32[8,5,64,8]{2,3,1,0:T(8,128)S(1)} all-gather(f32[2,5,64,8]{2,3,1,0:T(8,128)S(1)} %pad_maximum_fusion.11), channel_id=3, replica_groups=mesh['axial'=4,'azim'=32] {'axial'}, dimensions={0}, use_global_device_ids=true | all-gather | bytes 102400 | tf_op jit(solution)/shard_map/all_gather | solution.py:107
  255.0 12.3 %collective-permute-start.6 = (f32[5,64,3,128]{3,1,2,0:T(8,128)S(1)}, f32[5,64,3,128]{3,1,2,0:T(8,128)S(1)}, u32[]{:S(2)}, u32[]{:S(2)}) collective-permute-start(f32[5,64,3,128]{3,1,2,0:T(8,128)S(1)} %copy.26), channel_id=1, source_target_pairs={{1,0},{2,1},{3,2},{4,3},{5,4},{6,5},{7,6},{8,7},{9,8},{10,9},{11,1... | collective-permute-start | bytes 1474568 | tf_op jit(solution)/shard_map/ppermute | solution.py:28
  277.8 5.2 stack.103
  283.0 10.5 %all-to-all-start.1 = ((f32[32,1,2,5,64,128]{5,4,3,2,1,0:T(8,128)}), f32[32,1,2,5,64,128]{5,4,3,2,1,0:T(8,128)}, u32[]{:S(2)}, u32[]{:S(2)}) async-start(f32[32,1,2,5,64,128]{5,4,3,2,1,0:T(8,128)} %stack.103), calls=%async_computation.1 | async-start | bytes 20971520 | tf_op jit(solution)/shard_map/all_to_all | solution.py:146
  295.9 122.8 %all-to-all-done.1 = f32[32,1,2,5,64,128]{5,4,3,2,1,0:T(8,128)} async-done(((f32[32,1,2,5,64,128]{5,4,3,2,1,0:T(8,128)}), f32[32,1,2,5,64,128]{5,4,3,2,1,0:T(8,128)}, u32[]{:S(2)}, u32[]{:S(2)}) %all-to-all-start.1) | async-done | bytes 10485792 | tf_op jit(solution)/shard_map/all_to_all | solution.py:146
  418.8 5.2 slice_bitcast_fusion.1
  424.0 5.4 fusion.2
  429.4 5.6 fusion
  436.5 22.6 %scatter_custom_fusion = f32[65536]{0:T(1024)} fusion(s32[4096]{0:T(1024)S(1)} %add_bitcast_fusion, f32[4096]{0:T(1024)S(1)} %bitcast_multiply_fusion.21, f32[]{:T(128)} %constant.254.clone.1), kind=kCustom, calls=%fused_computation.160 | custom fusion | flops 4096 | bytes 262148 | tf_op jit(solution)/shard_map/scatter-add | solution.py:197
  459.2 145.3 %all-reduce.3.cloned.1.call-done = f32[512,128]{1,0:T(8,128)} async-done(((f32[512,128]{1,0:T(8,128)}), f32[512,128]{1,0:T(8,128)}) %all-reduce.3.cloned.1.call-update) | async-done | bytes 262160
  (130 shorter events, 64.2 us)
Async XLA Ops:
  7.2 286.4 %copy-start = (f32[256]{0:T(256)S(1)}, f32[256]{0:T(256)}, u32[]{:S(2)}) copy-start(f32[256]{0:T(256)} %param.23) | copy-start | bytes 3076
  11.8 33.2 %copy-start.12 = (f32[64,8,128]{2,1,0:T(8,128)}, f32[64,8,128]{2,1,0:T(8,128)S(1)}, u32[]{:S(2)}) copy-start(f32[64,8,128]{2,1,0:T(8,128)S(1)} %get-tuple-element.3) | copy-start | bytes 786436
  12.0 9.3 %collective-permute-start.2 = (f32[5,64,3,128]{3,1,2,0:T(8,128)S(1)}, f32[5,64,3,128]{3,1,2,0:T(8,128)S(1)}, u32[]{:S(2)}, u32[]{:S(2)}) collective-permute-start(f32[5,64,3,128]{3,1,2,0:T(8,128)S(1)} %copy.18), channel_id=1, source_target_pairs={{1,0},{2,1},{3,2},{4,3},{5,4},{6,5},{7,6},{8,7},{9,8},{10,9},{11,1... | collective-permute-start | bytes 1474568 | tf_op jit(solution)/shard_map/ppermute | solution.py:28
  13.6 8.1 %collective-permute-start.3 = (f32[5,64,3,128]{3,1,2,0:T(8,128)S(1)}, f32[5,64,3,128]{3,1,2,0:T(8,128)S(1)}, u32[]{:S(2)}, u32[]{:S(2)}) collective-permute-start(f32[5,64,3,128]{3,1,2,0:T(8,128)S(1)} %copy.20), channel_id=1, source_target_pairs={{0,1},{1,2},{2,3},{3,4},{4,5},{5,6},{6,7},{7,8},{8,9},{9,10},{10,1... | collective-permute-start | bytes 1474568 | tf_op jit(solution)/shard_map/ppermute | solution.py:26
  30.8 139.4 %all-to-all-start = ((f32[32,1,2,5,64,128]{5,4,3,2,1,0:T(8,128)}), f32[32,1,2,5,64,128]{5,4,3,2,1,0:T(8,128)}, u32[]{:S(2)}, u32[]{:S(2)}) async-start(f32[32,1,2,5,64,128]{5,4,3,2,1,0:T(8,128)} %stack.96), calls=%async_computation | async-start | bytes 20971520 | tf_op jit(solution)/shard_map/all_to_all | solution.py:146
  48.3 9.1 %collective-permute-start = (f32[5,64,8,3]{1,2,3,0:T(8,128)S(1)}, f32[5,64,8,3]{1,2,3,0:T(8,128)S(1)}, u32[]{:S(2)}, u32[]{:S(2)}) collective-permute-start(f32[5,64,8,3]{1,2,3,0:T(8,128)S(1)} %copy.14), channel_id=1, source_target_pairs={{32,0},{64,32},{96,64},{33,1},{65,33},{97,65},{34,2},{66,34},{98,6... | collective-permute-start | bytes 92168 | tf_op jit(solution)/shard_map/ppermute | solution.py:28
  50.7 8.3 %collective-permute-start.1 = (f32[5,64,8,3]{1,2,3,0:T(8,128)}, f32[5,64,8,3]{1,2,3,0:T(8,128)S(1)}, u32[]{:S(2)}, u32[]{:S(2)}) collective-permute-start(f32[5,64,8,3]{1,2,3,0:T(8,128)} %copy.16), channel_id=1, source_target_pairs={{0,32},{32,64},{64,96},{1,33},{33,65},{65,97},{2,34},{34,66},{66,9... | collective-permute-start | bytes 92168 | tf_op jit(solution)/shard_map/ppermute | solution.py:26
  175.4 11.1 %copy-start.21 = (f32[5,64,8,128]{3,2,1,0:T(8,128)S(1)}, f32[5,64,8,128]{3,2,1,0:T(8,128)}, u32[]{:S(2)}) copy-start(f32[5,64,8,128]{3,2,1,0:T(8,128)} %fusion.19) | copy-start | bytes 3932164
  180.9 5.7 copy-start.3
  180.9 5.7 copy-start.5
  180.9 5.7 copy-start.10
  180.9 5.7 copy-start.13
  180.9 5.7 copy-start.14
  180.9 5.7 copy-start.18
  191.7 5.8 collective-permute-start.4
  193.5 5.6 collective-permute-start.5
  255.0 13.8 %collective-permute-start.6 = (f32[5,64,3,128]{3,1,2,0:T(8,128)S(1)}, f32[5,64,3,128]{3,1,2,0:T(8,128)S(1)}, u32[]{:S(2)}, u32[]{:S(2)}) collective-permute-start(f32[5,64,3,128]{3,1,2,0:T(8,128)S(1)} %copy.26), channel_id=1, source_target_pairs={{1,0},{2,1},{3,2},{4,3},{5,4},{6,5},{7,6},{8,7},{9,8},{10,9},{11,1... | collective-permute-start | bytes 1474568 | tf_op jit(solution)/shard_map/ppermute | solution.py:28
  267.4 5.8 collective-permute-start.7
  283.0 10.6 %copy-start.19 = (s32[4,8,128]{2,1,0:T(8,128)S(1)}, s32[4,8,128]{2,1,0:T(8,128)}, u32[]{:S(2)}) copy-start(s32[4,8,128]{2,1,0:T(8,128)} %param.22) | copy-start | bytes 49156
  283.0 12.9 %copy-start.15 = (s32[4,8,128]{2,1,0:T(8,128)S(1)}, s32[4,8,128]{2,1,0:T(8,128)}, u32[]{:S(2)}) copy-start(s32[4,8,128]{2,1,0:T(8,128)} %param.21) | copy-start | bytes 49156
  283.0 12.9 %copy-start.16 = (s32[4,8,128]{2,1,0:T(8,128)S(1)}, s32[4,8,128]{2,1,0:T(8,128)}, u32[]{:S(2)}) copy-start(s32[4,8,128]{2,1,0:T(8,128)} %param.20) | copy-start | bytes 49156
  283.0 135.8 %all-to-all-start.1 = ((f32[32,1,2,5,64,128]{5,4,3,2,1,0:T(8,128)}), f32[32,1,2,5,64,128]{5,4,3,2,1,0:T(8,128)}, u32[]{:S(2)}, u32[]{:S(2)}) async-start(f32[32,1,2,5,64,128]{5,4,3,2,1,0:T(8,128)} %stack.103), calls=%async_computation.1 | async-start | bytes 20971520 | tf_op jit(solution)/shard_map/all_to_all | solution.py:146
  293.5 310.9 %all-reduce.3.cloned.1.call-start = ((), (), s32[]{:S(2)}) async-start(), calls=%async_computation.2 | async-start | bytes 524288
  436.5 169.2 %copy-start.11 = (f32[5,64,8,128]{3,2,1,0:T(8,128)}, f32[5,64,8,128]{3,2,1,0:T(8,128)S(1)}, u32[]{:S(2)}) copy-start(f32[5,64,8,128]{3,2,1,0:T(8,128)S(1)} %fusion.17) | copy-start | bytes 3932164
  (9 other events, 20.7 us)
Sparse Core Ops, SparseCore 0:
  459.3 145.1 all-reduce.2
